TPU v7x, 256 devices: a whole 4x4x8 slice. The times are simulated.
256 devices in a mesh: row: 8 (over y, core), col: 8 (over z), track: 4 (over x).
Axes of the slice: x: 4, y: 4, z: 8, core: 2. Of those that a mesh axis runs over, the one named last changes fastest.
Arguments:
- factors: float32 [16384, 2, 16, 576], P(('row', 'col', 'track')), may hold values from -0.5 to 0.5
- track_clusters: int32 [16384, 2], P(('row', 'col', 'track')), may hold values from 0 to 7, as said below
- filed_flip: int32 [16384], P(('row', 'col', 'track')), may hold values from 0 to 1, as said below
- damping: float32 [8, 576], P('row'), may hold values from 50 to 500
- rhs: float32 [8, 576], P('row'), may hold values from -3000 to 3000
Outputs:
- solution: float32 [8, 576], P('row')
- scaled_residual: float32 [8, 576], P('row')
- filed_blocks: float32 [8, 8, 576, 576], P('row', 'col', 'track')
Inputs may be any that keep to these rules, and one draw needn't show every extreme that they name: `track_clusters`: each row names two different clusters, the first below the second. `filed_flip`: the owner of a block filed under (i, j) is the device of row group i // 1 and column j, with the track index of the device that holds the track block. Of the 64 track blocks of one device at most 3 go to any one owner, and in every draw, for each track index, some owner receives exactly 3 from every device of that track index.
All inputs are finite; a program needn't handle non-finite values.
Results may differ from a plain program's by a relative error of at most 0.0003.
Values sent between devices are 32-bit elements; how exact they have to be, the bound alone decides.
No kernel may reach another device: no remote copies, remote signals or barrier semaphores. Data moves between devices by JAX's collectives and lax.ppermute only.
A program may use at most 128 MiB of HBM per device.

v0:
```python
import jax
import jax.numpy as jnp
from jax import lax
from jax.sharding import PartitionSpec as P

ITERS = 2
highest = lax.Precision.HIGHEST


def fitness_sum(residual, scaled):
    return lax.psum(jnp.sum(residual * scaled), "row")


def on_device(factors, track_clusters, filed_flip, damping, rhs):
    n_row = lax.axis_size("row")
    n_col = lax.axis_size("col")
    n_track = lax.axis_size("track")
    owners = n_row * n_col
    tb_dev = factors.shape[0]
    jac_rows = factors.shape[2]
    params = factors.shape[3]
    row_clusters = damping.shape[0]
    clusters = row_clusters * n_row
    capacity = 3 * tb_dev // owners
    row_share = params // n_track
    row_id = lax.axis_index("row")
    col_id = lax.axis_index("col")
    track_id = lax.axis_index("track")
    low_cluster = track_clusters[:, 0]
    high_cluster = track_clusters[:, 1]
    low_side = factors[:, 0]
    high_side = factors[:, 1]
    cluster_ids = jnp.arange(clusters, dtype=jnp.int32)
    low_onehot = (low_cluster[:, None] == cluster_ids[None, :]).astype(jnp.float32)
    high_onehot = (high_cluster[:, None] == cluster_ids[None, :]).astype(jnp.float32)
    diag_part = jnp.dot(low_onehot.T, jnp.sum(low_side * low_side, axis=1), precision=highest)
    diag_part = diag_part + jnp.dot(
        high_onehot.T, jnp.sum(high_side * high_side, axis=1), precision=highest
    )
    diag_all = lax.psum(diag_part, ("row", "col", "track"))
    precond = damping + lax.dynamic_slice_in_dim(diag_all, row_id * row_clusters, row_clusters, 0)
    flipped = filed_flip == 1
    filed_row = jnp.where(flipped, high_cluster, low_cluster)
    filed_col = jnp.where(flipped, low_cluster, high_cluster)
    oriented = jnp.where(flipped[:, None, None, None], factors[:, ::-1], factors)
    owner_row = filed_row // row_clusters
    target = owner_row * n_col + filed_col
    slot_ids = filed_row - owner_row * row_clusters
    owner_hits = (target[:, None] == jnp.arange(owners, dtype=jnp.int32)[None, :]).astype(jnp.int32)
    places = jnp.sum((jnp.cumsum(owner_hits, axis=0) - 1) * owner_hits, axis=1)
    position = target * capacity + places
    outgoing = (
        jnp.zeros((owners * capacity, 2, jac_rows, params), jnp.float32).at[position].set(oriented)
    )
    outgoing_slots = jnp.zeros((owners * capacity,), jnp.int32).at[position].set(slot_ids)
    incoming, incoming_slots = (
        lax.all_to_all(
            outgoing.reshape(owners, capacity, 2, jac_rows, params),
            ("row", "col"),
            split_axis=0,
            concat_axis=0,
            tiled=True,
        ),
        lax.all_to_all(
            outgoing_slots.reshape(owners, capacity),
            ("row", "col"),
            split_axis=0,
            concat_axis=0,
            tiled=True,
        ),
    )
    received = incoming.reshape(owners * capacity, 2, jac_rows, params)
    received_slots = incoming_slots.reshape(owners * capacity)
    received_rows = received[:, 0]
    received_cols = received[:, 1]
    slot_masks = [(received_slots == 0).astype(jnp.float32)]
    pieces = [
        jnp.einsum(
            "mkr,mkc->rc",
            received_rows * slot_mask[:, None, None],
            received_cols,
            precision=highest,
            preferred_element_type=jnp.float32,
        )
        for slot_mask in slot_masks
    ]
    filed = lax.psum_scatter(pieces[0], "track", scatter_dimension=0, tiled=True)
    filed_blocks = filed.reshape(row_share, row_clusters, params)
    blocks_out = jnp.transpose(filed_blocks, (1, 0, 2))[:, None]
    col_onehot = (cluster_ids == col_id).astype(jnp.float32)
    solution = jnp.zeros_like(rhs)
    residual = rhs
    scaled = residual / precond
    direction = scaled
    fitness = fitness_sum(residual, scaled)
    for iteration in range(ITERS):
        full_dir = lax.all_gather(direction, "row", axis=0, tiled=True)
        col_dir = jnp.dot(col_onehot, full_dir, precision=highest)
        own_share = lax.dynamic_slice_in_dim(direction, track_id * row_share, row_share, 1)
        row_terms = jnp.einsum("rsc,c->sr", filed_blocks, col_dir, precision=highest)
        col_terms = jnp.einsum("rsc,sr->c", filed_blocks, own_share, precision=highest)
        low_dir = jnp.dot(low_onehot, full_dir, precision=highest)
        high_dir = jnp.dot(high_onehot, full_dir, precision=highest)
        low_proj = jnp.einsum("mkc,mc->mk", low_side, low_dir, precision=highest)
        high_proj = jnp.einsum("mkc,mc->mk", high_side, high_dir, precision=highest)
        low_back = jnp.einsum("mk,mkc->mc", low_proj, low_side, precision=highest)
        high_back = jnp.einsum("mk,mkc->mc", high_proj, high_side, precision=highest)
        local = jnp.dot(low_onehot.T, low_back, precision=highest) + jnp.dot(
            high_onehot.T, high_back, precision=highest
        )
        placed = lax.dynamic_update_slice(
            jnp.zeros((clusters, params), jnp.float32),
            row_terms,
            (row_id * row_clusters, track_id * row_share),
        )
        local = local + placed + col_onehot[:, None] * col_terms[None, :]
        summed = lax.psum(local, ("row", "col", "track"))
        images = (
            lax.dynamic_slice_in_dim(summed, row_id * row_clusters, row_clusters, 0)
            + damping * direction
        )
        curvature = lax.psum(jnp.sum(direction * images), "row")
        images, curvature = (images, curvature)
        step_size = fitness / curvature
        solution = solution + step_size * direction
        residual = residual - step_size * images
        scaled = residual / precond
        fitness_next = fitness_sum(residual, scaled)
        direction = scaled + fitness_next / fitness * direction
        fitness = fitness_next
    return (solution, scaled, blocks_out)


def solution(mesh):
    in_specs = (
        P(("row", "col", "track"), None, None, None),
        P(("row", "col", "track"), None),
        P(("row", "col", "track")),
        P("row", None),
        P("row", None),
    )
    out_specs = (P("row", None), P("row", None), P("row", "col", "track", None))
    return jax.shard_map(
        on_device, mesh=mesh, in_specs=in_specs, out_specs=out_specs, check_vma=False
    )
```

profile of v0, /device:TPU:1, one launch (start us, length us, event | category | flops | bytes accessed | tf_op | source)
XLA Modules:
  0.0 1023.1 jit_solution(7229425490721513363)
XLA Ops:
  7.2 0.8 select_add_fusion
  8.3 0.8 scatter_custom_fusion.1
  9.1 0.8 all_to_all.10
  9.8 13.1 %all-to-all-start.1 = ((s32[64,1,3]{2,1,0:T(1,128)}), s32[64,1,3]{2,1,0:T(1,128)S(1)}, u32[]{:S(2)}, u32[]{:S(2)}) async-start(s32[64,1,3]{2,1,0:T(1,128)} %bitcast.21), calls=%async_computation.1 | async-start | bytes 65536 | tf_op jit(solution)/shard_map/all_to_all | solution.py:64
  23.0 0.7 broadcast_compare_fusion
  23.7 6.9 reverse_select_fusion
  30.5 7.5 broadcast_in_dim.12
  38.0 13.0 %scatter_fusion = f32[192,2,16,576]{3,2,1,0:T(8,128)} fusion(f32[192,2,16,576]{3,2,1,0:T(8,128)} %broadcast_in_dim.12, s32[64]{0:T(128)S(1)} %compare_select_fusion, f32[64,2,16,576]{3,2,1,0:T(8,128)} %reverse_select_fusion), kind=kCustom, calls=%fused_computation | custom fusion | bytes 14156032 | tf_op jit(solution)/shard_map/scatter | solution.py:53
  51.1 10.7 %all-to-all-start = ((f32[64,3,2,16,576]{4,3,2,1,0:T(8,128)}), f32[64,3,2,16,576]{4,3,2,1,0:T(8,128)}, u32[]{:S(2)}, u32[]{:S(2)}) async-start(f32[64,3,2,16,576]{4,3,2,1,0:T(8,128)} %bitcast.149), calls=%async_computation | async-start | bytes 31457280 | tf_op jit(solution)/shard_map/all_to_all | solution.py:57
  61.9 3.6 fusion.11
  65.4 0.3 fusion.60
  66.0 344.5 %all-to-all-done = f32[64,3,2,16,576]{4,3,2,1,0:T(8,128)} async-done(((f32[64,3,2,16,576]{4,3,2,1,0:T(8,128)}), f32[64,3,2,16,576]{4,3,2,1,0:T(8,128)}, u32[]{:S(2)}, u32[]{:S(2)}) %all-to-all-start) | async-done | bytes 14155808 | tf_op jit(solution)/shard_map/all_to_all | solution.py:57
  410.5 3.8 slice.25
  414.2 3.8 fusion
  418.1 247.6 %fusion.29 = f32[576,576]{1,0:T(8,128)} fusion(f32[192,1,16,576]{3,2,1,0:T(8,128)S(1)} %slice.25, f32[192,16,576]{2,1,0:T(8,128)S(1)} %fusion), kind=kOutput, calls=%fused_computation.36 | convolution fusion | flops 12230590464 | bytes 15482880 | tf_op jit(solution)/shard_map/mkr,mkc->rc/dot_general | solution.py:78
  665.7 0.3 convolution_add_fusion.2
  666.0 89.9 %psum.49 = f32[8,576]{1,0:T(8,128)S(1)} all-reduce(f32[8,576]{1,0:T(8,128)S(1)} %convolution_add_fusion.2), channel_id=1, replica_groups=mesh['row'=8,'col'=8,'track'=4] {'row','col','track'}, use_global_device_ids=true, to_apply=%region_2.0 | all-reduce | flops 4608 | bytes 36864 | tf_op jit(solution)/shard_map/psum | solution.py:40
  755.9 13.4 %all-gather = f32[8,1,576]{2,1,0:T(1,128)S(1)} all-gather(f32[1,1,576]{2,1,0:T(1,128)S(1)} %bitcast.151), channel_id=1, replica_groups=mesh['row'=8,'col'=8,'track'=4] {'row'}, dimensions={0}, use_global_device_ids=true | all-gather | bytes 20736 | tf_op jit(solution)/shard_map/all_gather | solution.py:97
  769.4 0.3 convolution_bitcast_fusion.3
  769.6 0.3 convolution_bitcast_fusion.2
  770.0 5.1 fusion.32
  775.2 3.3 fusion.16
  778.5 0.3 fusion.48
  778.7 5.1 fusion.38
  783.9 3.4 fusion.7
  787.2 0.3 convolution_add_fusion.1
  787.6 1.4 convolution_add_fusion.4
  789.2 1.3 convolution_reduce_fusion.1
  790.7 73.0 %psum.51 = f32[8,576]{1,0:T(8,128)S(1)} all-reduce(f32[8,576]{1,0:T(8,128)S(1)} %multiply_add_fusion.1), channel_id=1, replica_groups=mesh['row'=8,'col'=8,'track'=4] {'row','col','track'}, use_global_device_ids=true, to_apply=%region_10.11 | all-reduce | flops 4608 | bytes 36864 | tf_op jit(solution)/shard_map/psum | solution.py:117
  863.6 0.6 multiply_reduce_fusion.2
  864.3 13.1 %all-reduce = (f32[]{:T(128)}, f32[]{:T(128)}) all-reduce(f32[]{:T(128)} %get-tuple-element.6, f32[]{:T(128)} %get-tuple-element.5), channel_id=1, replica_groups=mesh['row'=8,'col'=8,'track'=4] {'row'}, use_global_device_ids=true, to_apply=%region_4.5 | all-reduce | flops 2 | bytes 16 | tf_op jit(solution)/shard_map/psum | solution.py:11
  878.7 0.6 multiply_reduce_fusion.1
  879.3 15.3 %psum.53 = f32[]{:T(128)} all-reduce(f32[]{:T(128)} %get-tuple-element.9), channel_id=1, replica_groups=mesh['row'=8,'col'=8,'track'=4] {'row'}, use_global_device_ids=true, to_apply=%region_14.15 | all-reduce | flops 1 | bytes 8 | tf_op jit(solution)/shard_map/psum | solution.py:11
  895.9 13.4 %all-gather.1 = f32[8,1,576]{2,1,0:T(1,128)S(1)} all-gather(f32[1,1,576]{2,1,0:T(1,128)S(1)} %bitcast.152), channel_id=1, replica_groups=mesh['row'=8,'col'=8,'track'=4] {'row'}, dimensions={0}, use_global_device_ids=true | all-gather | bytes 20736 | tf_op jit(solution)/shard_map/all_gather | solution.py:97
  909.3 0.3 convolution_bitcast_fusion.1
  909.6 0.3 convolution_bitcast_fusion
  910.0 5.3 fusion.35
  915.3 3.3 fusion.12
  918.6 0.3 fusion.45
  918.9 5.1 fusion.41
  924.0 1.5 fusion.3
  925.6 0.3 convolution_add_fusion
  925.9 0.4 convolution_add_fusion.3
  926.5 0.4 convolution_reduce_fusion
  927.0 73.7 %psum.54 = f32[8,576]{1,0:T(8,128)S(1)} all-reduce(f32[8,576]{1,0:T(8,128)S(1)} %multiply_add_fusion), channel_id=1, replica_groups=mesh['row'=8,'col'=8,'track'=4] {'row','col','track'}, use_global_device_ids=true, to_apply=%region_15.16 | all-reduce | flops 4608 | bytes 36864 | tf_op jit(solution)/shard_map/psum | solution.py:117
  1000.7 0.6 multiply_reduce_fusion
  1001.3 13.1 %psum.55 = f32[]{:T(128)} all-reduce(f32[]{:T(128)} %multiply_reduce_fusion), channel_id=1, replica_groups=mesh['row'=8,'col'=8,'track'=4] {'row'}, use_global_device_ids=true, to_apply=%region_17.18 | all-reduce | flops 1 | bytes 8 | tf_op jit(solution)/shard_map/psum | solution.py:122
  1015.7 0.6 subtract_divide_fusion
  (34 shorter events, 1.6 us)
Async XLA Ops:
  9.8 41.2 %all-to-all-start.1 = ((s32[64,1,3]{2,1,0:T(1,128)}), s32[64,1,3]{2,1,0:T(1,128)S(1)}, u32[]{:S(2)}, u32[]{:S(2)}) async-start(s32[64,1,3]{2,1,0:T(1,128)} %bitcast.21), calls=%async_computation.1 | async-start | bytes 65536 | tf_op jit(solution)/shard_map/all_to_all | solution.py:64
  51.0 10.8 %copy-start.3 = (s32[64,2]{0,1:T(2,128)S(1)}, s32[64,2]{0,1:T(2,128)}, u32[]{:S(2)}) copy-start(s32[64,2]{0,1:T(2,128)} %param.6) | copy-start | bytes 1540
  51.1 359.4 %all-to-all-start = ((f32[64,3,2,16,576]{4,3,2,1,0:T(8,128)}), f32[64,3,2,16,576]{4,3,2,1,0:T(8,128)}, u32[]{:S(2)}, u32[]{:S(2)}) async-start(f32[64,3,2,16,576]{4,3,2,1,0:T(8,128)} %bitcast.149), calls=%async_computation | async-start | bytes 31457280 | tf_op jit(solution)/shard_map/all_to_all | solution.py:57
  61.8 725.8 %reduce-scatter.2.cloned.1.call-start = ((), (), s32[]{:S(2)}) async-start(), calls=%async_computation.3 | async-start | bytes 1843200 | tf_op jit(solution)/shard_map/reduce_scatter | solution.py:87
  418.1 337.9 %copy-start.1 = (f32[1,576]{1,0:T(1,128)S(1)}, f32[1,576]{1,0:T(1,128)}, u32[]{:S(2)}) copy-start(f32[1,576]{1,0:T(1,128)} %param.8) | copy-start | bytes 6916
  418.1 337.8 %copy-start.2 = (f32[1,576]{1,0:T(1,128)S(1)}, f32[1,576]{1,0:T(1,128)}, u32[]{:S(2)}) copy-start(f32[1,576]{1,0:T(1,128)} %param.9) | copy-start | bytes 6916
  783.9 140.1 %slice-start = ((s8[5242880]{0:T(1024)(128)(4,1)}), s8[1048576]{0:T(1024)(128)(4,1)S(1)}, s32[]{:S(2)}) async-start(s8[5242880]{0:T(1024)(128)(4,1)} %bitcast.147), calls=%async_computation.4 | async-start | bytes 2097152
  910.0 14.0 %slice-start.1 = ((s8[5242880]{0:T(1024)(128)(4,1)}), s8[4194304]{0:T(1024)(128)(4,1)S(1)}, s32[]{:S(2)}) async-start(s8[5242880]{0:T(1024)(128)(4,1)} %bitcast.147), calls=%async_computation.5 | async-start | bytes 8388608
  910.0 15.8 %copy-start = (f32[144,576]{1,0:T(8,128)S(1)}, f32[144,576]{1,0:T(8,128)}, u32[]{:S(2)}) copy-start(f32[144,576]{1,0:T(8,128)} %reduce-scatter.2.cloned.1.call-done) | copy-start | bytes 995332
Sparse Core Ops, SparseCore 0:
  665.8 38.9 reduce-scatter.1
where the time goes:
time: 1020 us
  waiting for transfers between devices  345 us (34%)
  blocking collectives  305 us (30%)
  matrix products  286 us (28%)
  local copies, waits for them, and re-layouts  26.5 us (3%)
  starting transfers between devices  23.9 us (2%)
  other arithmetic  18.8 us (2%)
  between operations  18.3 us (2%)
    all_to_all x1, waiting for transfers between devices, on_device(): lax.all_to_all(outgoing.reshape(owners, capacity, 2, jac_rows, params), (...  345 us
    dot_general x1, matrix products, on_device(): jnp.einsum('mkr,mkc->rc', received_rows * slot_mask[:, None, None], recei...  248 us
    psum x2, blocking collectives, on_device(): summed = lax.psum(local, ('row', 'col', 'track'))  147 us
    psum x1, blocking collectives, on_device(): diag_all = lax.psum(diag_part, ('row', 'col', 'track'))  89.9 us
    psum x2, blocking collectives, fitness_sum(): return lax.psum(jnp.sum(residual * scaled), 'row')  28.3 us
    all_gather x2, blocking collectives, on_device(): full_dir = lax.all_gather(direction, 'row', axis=0, tiled=True)  26.8 us
  transfers between devices with their start and end apart: 3, of which 1 were waited for; matrix products, arithmetic and copies ran while one was open for 5% of the time, Pallas kernels for 0%

commit v1 on v0

--- a/solution.py
+++ b/solution.py
@@ -114,7 +114,7 @@
             (row_id * row_clusters, track_id * row_share),
         )
         local = local + placed + col_onehot[:, None] * col_terms[None, :]
-        summed = lax.psum(local, ("row", "col", "track"))
+        summed = jax.lax.psum(jax.lax.psum(local, "row"), ("col", "track"))
         images = (
             lax.dynamic_slice_in_dim(summed, row_id * row_clusters, row_clusters, 0)
             + damping * direction

time: 1020 us -> 1200 us (1.18)
  blocking collectives: 305 us -> 479 us
    psum x2 -> x4, blocking collectives: 147 us -> 263 us  [on_device(): summed = jax.lax.psum(jax.lax.psum(local, 'row'), ('col', 'track'))]
    psum x1, blocking collectives: 13.1 us -> 43.2 us  [on_device(): curvature = lax.psum(jnp.sum(direction * images), 'row')]
    psum x2, blocking collectives: 28.3 us -> 56.3 us  [fitness_sum(): return lax.psum(jnp.sum(residual * scaled), 'row')]
  transfers between devices with their start and end apart: 3 -> 3, of which waited for: 1 -> 1; matrix products, arithmetic and copies ran while one was open for 5% -> 4% of each run, Pallas kernels for 0% -> 0%
where the time goes in v1:
time: 1200 us
  blocking collectives  479 us (40%)
  waiting for transfers between devices  345 us (29%)
  matrix products  286 us (24%)
  local copies, waits for them, and re-layouts  26.5 us (2%)
  starting transfers between devices  23.9 us (2%)
  other arithmetic  18.8 us (2%)
  between operations  18.3 us (2%)
    all_to_all x1, waiting for transfers between devices, on_device(): lax.all_to_all(outgoing.reshape(owners, capacity, 2, jac_rows, params), (...  345 us
    psum x4, blocking collectives, on_device(): summed = jax.lax.psum(jax.lax.psum(local, 'row'), ('col', 'track'))  263 us
    dot_general x1, matrix products, on_device(): jnp.einsum('mkr,mkc->rc', received_rows * slot_mask[:, None, None], recei...  248 us
    psum x1, blocking collectives, on_device(): diag_all = lax.psum(diag_part, ('row', 'col', 'track'))  89.9 us
    psum x2, blocking collectives, fitness_sum(): return lax.psum(jnp.sum(residual * scaled), 'row')  56.3 us
    psum x1, blocking collectives, on_device(): curvature = lax.psum(jnp.sum(direction * images), 'row')  43.2 us
    all_gather x2, blocking collectives, on_device(): full_dir = lax.all_gather(direction, 'row', axis=0, tiled=True)  26.8 us
  transfers between devices with their start and end apart: 3, of which 1 were waited for; matrix products, arithmetic and copies ran while one was open for 4% of the time, Pallas kernels for 0%

profile of v1, /device:TPU:1, one launch (start us, length us, event | category | flops | bytes accessed | tf_op | source)
XLA Modules:
  0.0 1197.7 jit_solution(5563441984257847334)
XLA Ops:
  7.2 0.8 select_add_fusion
  8.3 0.8 scatter_custom_fusion.1
  9.1 0.8 all_to_all.10
  9.8 13.1 %all-to-all-start.1 = ((s32[64,1,3]{2,1,0:T(1,128)}), s32[64,1,3]{2,1,0:T(1,128)S(1)}, u32[]{:S(2)}, u32[]{:S(2)}) async-start(s32[64,1,3]{2,1,0:T(1,128)} %bitcast.21), calls=%async_computation.1 | async-start | bytes 65536 | tf_op jit(solution)/shard_map/all_to_all | solution.py:64
  23.0 0.7 broadcast_compare_fusion
  23.7 6.9 reverse_select_fusion
  30.5 7.5 broadcast_in_dim.12
  38.0 13.0 %scatter_fusion = f32[192,2,16,576]{3,2,1,0:T(8,128)} fusion(f32[192,2,16,576]{3,2,1,0:T(8,128)} %broadcast_in_dim.12, s32[64]{0:T(128)S(1)} %compare_select_fusion, f32[64,2,16,576]{3,2,1,0:T(8,128)} %reverse_select_fusion), kind=kCustom, calls=%fused_computation | custom fusion | bytes 14156032 | tf_op jit(solution)/shard_map/scatter | solution.py:53
  51.1 10.7 all-to-all-start
  61.9 3.6 fusion.11
  65.4 0.3 fusion.60
  66.0 344.5 %all-to-all-done = f32[64,3,2,16,576]{4,3,2,1,0:T(8,128)} async-done(((f32[64,3,2,16,576]{4,3,2,1,0:T(8,128)}), f32[64,3,2,16,576]{4,3,2,1,0:T(8,128)}, u32[]{:S(2)}, u32[]{:S(2)}) %all-to-all-start) | async-done | bytes 14155808 | tf_op jit(solution)/shard_map/all_to_all | solution.py:57
  410.5 3.8 slice.25
  414.2 3.8 fusion
  418.1 247.6 %fusion.29 = f32[576,576]{1,0:T(8,128)} fusion(f32[192,1,16,576]{3,2,1,0:T(8,128)S(1)} %slice.25, f32[192,16,576]{2,1,0:T(8,128)S(1)} %fusion), kind=kOutput, calls=%fused_computation.36 | convolution fusion | flops 12230590464 | bytes 15482880 | tf_op jit(solution)/shard_map/mkr,mkc->rc/dot_general | solution.py:78
  665.7 0.3 convolution_add_fusion.2
  666.0 89.9 %psum.63 = f32[8,576]{1,0:T(8,128)S(1)} all-reduce(f32[8,576]{1,0:T(8,128)S(1)} %convolution_add_fusion.2), channel_id=1, replica_groups=mesh['row'=8,'col'=8,'track'=4] {'row','col','track'}, use_global_device_ids=true, to_apply=%region_2.0 | all-reduce | flops 4608 | bytes 36864 | tf_op jit(solution)/shard_map/psum | solution.py:40
  755.9 13.4 %all-gather = f32[8,1,576]{2,1,0:T(1,128)S(1)} all-gather(f32[1,1,576]{2,1,0:T(1,128)S(1)} %bitcast.151), channel_id=1, replica_groups=mesh['row'=8,'col'=8,'track'=4] {'row'}, dimensions={0}, use_global_device_ids=true | all-gather | bytes 20736 | tf_op jit(solution)/shard_map/all_gather | solution.py:97
  769.4 0.3 convolution_bitcast_fusion.3
  770.0 5.1 fusion.32
  775.2 3.3 fusion.16
  778.5 0.3 fusion.48
  778.7 5.1 fusion.38
  783.9 3.4 fusion.7
  787.2 0.3 convolution_add_fusion.1
  787.6 1.4 convolution_add_fusion.4
  789.2 1.3 convolution_reduce_fusion.1
  790.7 22.1 %psum.65 = f32[8,576]{1,0:T(8,128)S(1)} all-reduce(f32[8,576]{1,0:T(8,128)S(1)} %multiply_add_fusion.1), channel_id=1, replica_groups=mesh['row'=8,'col'=8,'track'=4] {'row'}, use_global_device_ids=true, to_apply=%region_10.11 | all-reduce | flops 4608 | bytes 36864 | tf_op jit(solution)/shard_map/psum | solution.py:117
  812.7 110.4 %psum.66 = f32[8,576]{1,0:T(8,128)S(1)} all-reduce(f32[8,576]{1,0:T(8,128)S(1)} %psum.65), channel_id=1, replica_groups=mesh['row'=8,'col'=8,'track'=4] {'col','track'}, use_global_device_ids=true, to_apply=%region_11.12 | all-reduce | flops 4608 | bytes 36864 | tf_op jit(solution)/shard_map/psum | solution.py:117
  923.1 0.6 multiply_reduce_fusion.2
  923.7 43.3 %all-reduce = (f32[]{:T(128)}, f32[]{:T(128)}) all-reduce(f32[]{:T(128)} %get-tuple-element.6, f32[]{:T(128)} %get-tuple-element.5), channel_id=1, replica_groups=mesh['row'=8,'col'=8,'track'=4] {'row'}, use_global_device_ids=true, to_apply=%region_4.5 | all-reduce | flops 2 | bytes 16 | tf_op jit(solution)/shard_map/psum | solution.py:11
  968.3 0.6 multiply_reduce_fusion.1
  968.9 13.0 %psum.68 = f32[]{:T(128)} all-reduce(f32[]{:T(128)} %get-tuple-element.9), channel_id=1, replica_groups=mesh['row'=8,'col'=8,'track'=4] {'row'}, use_global_device_ids=true, to_apply=%region_15.16 | all-reduce | flops 1 | bytes 8 | tf_op jit(solution)/shard_map/psum | solution.py:11
  983.3 13.4 %all-gather.1 = f32[8,1,576]{2,1,0:T(1,128)S(1)} all-gather(f32[1,1,576]{2,1,0:T(1,128)S(1)} %bitcast.152), channel_id=1, replica_groups=mesh['row'=8,'col'=8,'track'=4] {'row'}, dimensions={0}, use_global_device_ids=true | all-gather | bytes 20736 | tf_op jit(solution)/shard_map/all_gather | solution.py:97
  997.0 0.3 convolution_bitcast_fusion
  997.4 5.3 fusion.35
  1002.7 3.3 fusion.12
  1006.0 0.3 fusion.45
  1006.3 5.1 fusion.41
  1011.4 1.5 fusion.3
  1013.0 0.3 convolution_add_fusion
  1013.2 0.4 convolution_add_fusion.3
  1013.9 0.4 convolution_reduce_fusion
  1014.4 20.4 %psum.69 = f32[8,576]{1,0:T(8,128)S(1)} all-reduce(f32[8,576]{1,0:T(8,128)S(1)} %multiply_add_fusion), channel_id=1, replica_groups=mesh['row'=8,'col'=8,'track'=4] {'row'}, use_global_device_ids=true, to_apply=%region_16.17 | all-reduce | flops 4608 | bytes 36864 | tf_op jit(solution)/shard_map/psum | solution.py:117
  1034.7 110.4 %psum.70 = f32[8,576]{1,0:T(8,128)S(1)} all-reduce(f32[8,576]{1,0:T(8,128)S(1)} %psum.69), channel_id=1, replica_groups=mesh['row'=8,'col'=8,'track'=4] {'col','track'}, use_global_device_ids=true, to_apply=%region_17.18 | all-reduce | flops 4608 | bytes 36864 | tf_op jit(solution)/shard_map/psum | solution.py:117
  1145.1 0.6 multiply_reduce_fusion
  1145.7 43.2 %psum.71 = f32[]{:T(128)} all-reduce(f32[]{:T(128)} %multiply_reduce_fusion), channel_id=1, replica_groups=mesh['row'=8,'col'=8,'track'=4] {'row'}, use_global_device_ids=true, to_apply=%region_19.20 | all-reduce | flops 1 | bytes 8 | tf_op jit(solution)/shard_map/psum | solution.py:122
  1190.3 0.6 subtract_divide_fusion
  (36 shorter events, 2.1 us)
Async XLA Ops:
  9.8 41.2 %all-to-all-start.1 = ((s32[64,1,3]{2,1,0:T(1,128)}), s32[64,1,3]{2,1,0:T(1,128)S(1)}, u32[]{:S(2)}, u32[]{:S(2)}) async-start(s32[64,1,3]{2,1,0:T(1,128)} %bitcast.21), calls=%async_computation.1 | async-start | bytes 65536 | tf_op jit(solution)/shard_map/all_to_all | solution.py:64
  51.0 10.8 copy-start.3
  51.1 359.4 %all-to-all-start = ((f32[64,3,2,16,576]{4,3,2,1,0:T(8,128)}), f32[64,3,2,16,576]{4,3,2,1,0:T(8,128)}, u32[]{:S(2)}, u32[]{:S(2)}) async-start(f32[64,3,2,16,576]{4,3,2,1,0:T(8,128)} %bitcast.149), calls=%async_computation | async-start | bytes 31457280 | tf_op jit(solution)/shard_map/all_to_all | solution.py:57
  61.8 725.8 %reduce-scatter.2.cloned.1.call-start = ((), (), s32[]{:S(2)}) async-start(), calls=%async_computation.3 | async-start | bytes 1843200 | tf_op jit(solution)/shard_map/reduce_scatter | solution.py:87
  418.1 337.9 %copy-start.1 = (f32[1,576]{1,0:T(1,128)S(1)}, f32[1,576]{1,0:T(1,128)}, u32[]{:S(2)}) copy-start(f32[1,576]{1,0:T(1,128)} %param.8) | copy-start | bytes 6916
  418.1 337.8 %copy-start.2 = (f32[1,576]{1,0:T(1,128)S(1)}, f32[1,576]{1,0:T(1,128)}, u32[]{:S(2)}) copy-start(f32[1,576]{1,0:T(1,128)} %param.9) | copy-start | bytes 6916
  783.9 227.5 %slice-start = ((s8[5242880]{0:T(1024)(128)(4,1)}), s8[1048576]{0:T(1024)(128)(4,1)S(1)}, s32[]{:S(2)}) async-start(s8[5242880]{0:T(1024)(128)(4,1)} %bitcast.147), calls=%async_computation.4 | async-start | bytes 2097152
  997.4 14.0 %slice-start.1 = ((s8[5242880]{0:T(1024)(128)(4,1)}), s8[4194304]{0:T(1024)(128)(4,1)S(1)}, s32[]{:S(2)}) async-start(s8[5242880]{0:T(1024)(128)(4,1)} %bitcast.147), calls=%async_computation.5 | async-start | bytes 8388608
  997.4 15.8 %copy-start = (f32[144,576]{1,0:T(8,128)S(1)}, f32[144,576]{1,0:T(8,128)}, u32[]{:S(2)}) copy-start(f32[144,576]{1,0:T(8,128)} %reduce-scatter.2.cloned.1.call-done) | copy-start | bytes 995332
Sparse Core Ops, SparseCore 0:
  665.8 38.9 reduce-scatter.1
